TPU v7x, 32 devices: a whole 2x2x4 slice. The times are simulated.
32 devices in a mesh: slides: 2 (over x), tok: 16 (over z, y, core).
Axes of the slice: x: 2, y: 2, z: 4, core: 2. Of those that a mesh axis runs over, the one named last changes fastest.
Arguments:
- queries: bfloat16 [8, 2048, 768], P('slides', 'tok'), parts along dimension 0, may hold values from -7 to 7
- key_rows: bfloat16 [8, 2048, 768], P('slides', 'tok'), parts along dimension 0, may hold values from -6 to 6
- value_rows: bfloat16 [8, 2048, 768], P('slides', 'tok'), parts along dimension 0, may hold values from -6 to 6
- projected_output_gradient: bfloat16 [8, 32768, 768], P('slides', 'tok'), parts along dimension 0, may hold values from -24 to 24
- out_weight: bfloat16 [768, 768], replicated, may hold values from -0.21875 to 0.21875
- offsets: int32 [16], replicated, may hold values from 0 to 15, each once
Outputs:
- grad_queries: bfloat16 [8, 2048, 768], P('slides', 'tok'), parts along dimension 0
- grad_keys: bfloat16 [8, 2048, 768], P('slides', 'tok'), parts along dimension 0
- grad_values: bfloat16 [8, 2048, 768], P('slides', 'tok'), parts along dimension 0
- grad_weight: float32 [1536, 768], P(('slides', 'tok')), parts along dimension 0
There are 2 independent parts, one for each index of `slides`. A program takes and returns all parts, laid end to end along the dimension named above; an argument that names none is the same for every part. Nothing has to cross between parts.
Inputs may be any that keep to these rules, and one draw needn't show every extreme that they name: offsets names each of the 16 phases once.
All inputs are finite; a program needn't handle non-finite values.
Results may differ from a plain program's by a relative error of at most 0.014.
Values may be sent and summed in bfloat16 or wider, within the bound.
A program may use at most 192 MiB of HBM per device.

v0:
```python
import jax
import jax.numpy as jnp
from jax import lax
from jax.sharding import PartitionSpec as P


def shortened(array):
    return jax.tree.map(lambda a: a.astype(jnp.bfloat16) if a.dtype == jnp.float32 else a, array)


def attend(query_all, key_all, value_all, grad_all):
    seg_rows, head_dim = query_all.shape
    block_rows = min(512, seg_rows)
    score_scale = head_dim ** (-0.5)
    key_sum = jnp.zeros((seg_rows, head_dim), jnp.float32)
    value_sum = jnp.zeros((seg_rows, head_dim), jnp.float32)
    query_parts = []
    output_parts = []
    for first_row in range(0, seg_rows, block_rows):
        query_part = query_all[first_row : first_row + block_rows]
        grad_part = grad_all[first_row : first_row + block_rows]
        scores = (
            jnp.einsum("qe,ke->qk", query_part, key_all, preferred_element_type=jnp.float32)
            * score_scale
        )
        top_score = jnp.max(scores, axis=1, keepdims=True)
        expo = jnp.exp(scores - top_score)
        probs = expo / jnp.sum(expo, axis=1, keepdims=True)
        probs_low = probs.astype(jnp.bfloat16)
        attn_part = jnp.einsum(
            "qk,ke->qe", probs_low, value_all, preferred_element_type=jnp.float32
        ).astype(jnp.bfloat16)
        dprobs = jnp.einsum("qe,ke->qk", grad_part, value_all, preferred_element_type=jnp.float32)
        delta = jnp.sum(
            grad_part.astype(jnp.float32) * attn_part.astype(jnp.float32), axis=1, keepdims=True
        )
        dscores = (probs * (dprobs - delta)).astype(jnp.bfloat16)
        query_grad = (
            jnp.einsum("qk,ke->qe", dscores, key_all, preferred_element_type=jnp.float32)
            * score_scale
        )
        query_parts.append(query_grad.astype(jnp.bfloat16))
        output_parts.append(attn_part)
        key_sum = key_sum + jnp.einsum(
            "qk,qe->ke", dscores, query_part, preferred_element_type=jnp.float32
        )
        value_sum = value_sum + jnp.einsum(
            "qk,qe->ke", probs_low, grad_part, preferred_element_type=jnp.float32
        )
    grad_query = jnp.concatenate(query_parts, axis=0)
    grad_key = (key_sum * score_scale).astype(jnp.bfloat16)
    grad_value = value_sum.astype(jnp.bfloat16)
    attn_out = jnp.concatenate(output_parts, axis=0)
    return (grad_query, grad_key, grad_value, attn_out)


def local(queries, key_rows, value_rows, projected_output_gradient, out_weight, offsets):
    rounds, rows_dev, feature_width = queries.shape
    heads = offsets.shape[0]
    head_dim = feature_width // heads
    phase_offsets = projected_output_gradient.shape[1] // rows_dev
    flat_size = rows_dev * head_dim
    tok_count = lax.axis_size("tok")
    groups = tok_count // heads
    phase_shifted = projected_output_gradient.reshape(
        rounds, rows_dev, phase_offsets, feature_width
    )
    chosen = jnp.take(phase_shifted, offsets, axis=2)
    weight_split = out_weight.reshape(feature_width, heads, head_dim)
    grad_heads = jnp.einsum(
        "rihj,jhe->rihe", chosen, weight_split, preferred_element_type=jnp.float32
    ).astype(jnp.bfloat16)
    separated = jnp.stack(
        [
            queries.reshape(rounds, rows_dev, heads, head_dim),
            key_rows.reshape(rounds, rows_dev, heads, head_dim),
            value_rows.reshape(rounds, rows_dev, heads, head_dim),
            grad_heads,
        ],
        axis=1,
    )
    outgoing = separated.transpose(0, 3, 1, 2, 4).reshape(rounds, heads, 4, flat_size)

    def owner_work(arrived):
        group = arrived.shape[0]
        gathered = (
            arrived.reshape(group, 4, rows_dev, head_dim)
            .transpose(1, 0, 2, 3)
            .reshape(4, group * rows_dev, head_dim)
        )
        grad_query, grad_key, grad_value, attn_out = attend(
            gathered[0], gathered[1], gathered[2], gathered[3]
        )
        stacked = jnp.stack([grad_query, grad_key, grad_value, attn_out])
        return (
            stacked.reshape(4, group, rows_dev, head_dim)
            .transpose(1, 0, 2, 3)
            .reshape(group, 4, flat_size)
        )

    pieces = []
    for first_round in range(0, rounds, groups):
        block_rounds = outgoing[first_round : first_round + groups]
        block_count = block_rounds.shape[0]
        count = block_count // groups
        sending = (
            block_rounds.reshape(groups, count, heads, 4, flat_size)
            .transpose(0, 2, 1, 3, 4)
            .reshape(tok_count, count, 4, flat_size)
        )
        exchange_arrived = lax.all_to_all(sending, "tok", split_axis=0, concat_axis=0, tiled=True)
        items = (
            exchange_arrived.reshape(groups, heads, count, 4, flat_size)
            .transpose(0, 2, 1, 3, 4)
            .reshape(groups * count, heads, 4, flat_size)
        )
        results = lax.map(owner_work, items)
        results = (
            results.reshape(groups, count, heads, 4, flat_size)
            .transpose(0, 2, 1, 3, 4)
            .reshape(tok_count, count, 4, flat_size)
        )
        received = lax.all_to_all(
            shortened(results), "tok", split_axis=0, concat_axis=0, tiled=True
        ).astype(results.dtype)
        pieces.append(
            received.reshape(groups, heads, count, 4, flat_size)
            .transpose(0, 2, 1, 3, 4)
            .reshape(block_count, heads, 4, flat_size)
        )
    returned = jnp.concatenate(pieces, axis=0)
    laid_out = (
        returned.reshape(rounds, heads, 4, rows_dev, head_dim)
        .transpose(2, 0, 3, 1, 4)
        .reshape(4, rounds, rows_dev, feature_width)
    )
    grad_queries = laid_out[0]
    grad_keys = laid_out[1]
    grad_values = laid_out[2]
    attn_rows = laid_out[3].reshape(rounds, rows_dev, heads, head_dim)
    term = jnp.einsum("rihj,rihe->jhe", chosen, attn_rows, preferred_element_type=jnp.float32)
    grad_weight = lax.psum_scatter(
        term.reshape(feature_width // tok_count * lax.axis_size("tok"), feature_width),
        "tok",
        scatter_dimension=0,
        tiled=True,
    )
    return (grad_queries, grad_keys, grad_values, grad_weight)


def solution(mesh):
    placed = (
        P("slides", "tok", None),
        P("slides", "tok", None),
        P("slides", "tok", None),
        P("slides", "tok", None),
        P(),
        P(),
    )
    return jax.shard_map(
        local,
        mesh=mesh,
        in_specs=placed,
        out_specs=(
            P("slides", "tok", None),
            P("slides", "tok", None),
            P("slides", "tok", None),
            P(("slides", "tok"), None),
        ),
        check_vma=False,
    )
```

profile of v0, /device:TPU:0, one launch (start us, length us, event | category | flops | bytes accessed | tf_op | source)
XLA Modules:
  0.0 498.4 jit_solution(14149702405340478532)
XLA Ops:
  10.9 12.7 %copy.124 = bf16[4,128,16,768]{3,1,2,0:T(8,128)(2,1)} copy(bf16[4,128,16,768]{3,2,1,0:T(8,128)(2,1)} %bitcast.443) | data formatting | bytes 25165824 | tf_op jit(solution)/shard_map/reshape | solution.py:65
  24.8 11.1 %gather_fusion = bf16[16,4,128,768]{3,2,1,0:T(8,128)(2,1)} fusion(bf16[4,128,16,768]{3,1,2,0:T(8,128)(2,1)} %copy.124, s32[1024]{0:T(1024)S(1)} %pad_clamp_fusion), kind=kCustom, calls=%fused_computation | custom fusion | bytes 25165888 | tf_op jit(solution)/shard_map/jit(_take)/gather | solution.py:68
  35.8 8.8 %fusion.51 = bf16[4,1,128,16,48]{2,4,0,3,1:T(8,128)(2,1)S(1)} fusion(bf16[768,16,48,1]{0,2,3,1:T(8,128)(2,1)} %bitcast.539, bf16[16,4,128,768]{3,2,1,0:T(8,128)(2,1)} %gather_fusion, pred[16]{0:T(512)(128)(4,1)S(1)} %compare_and_fusion), kind=kOutput, calls=%fused_computation.125 | convolution fusion | flops 610664448 | bytes 14549008 | tf_op jit(solution)/shard_map/rihj,jhe->rihe/dot_general | solution.py:70
  48.8 3.7 reshape.276
  52.5 7.5 %all-to-all-start.6 = ((bf16[16,1,4,6144]{3,2,1,0:T(4,128)(2,1)}), bf16[16,1,4,6144]{3,2,1,0:T(4,128)(2,1)}, u32[]{:S(2)}, u32[]{:S(2)}) async-start(bf16[16,1,4,6144]{3,2,1,0:T(4,128)(2,1)} %reshape.276), calls=%async_computation.6 | async-start | bytes 1572864 | tf_op jit(solution)/shard_map/all_to_all | solution.py:111
  61.9 3.7 reshape.273
  65.6 13.1 %all-to-all-done.6 = bf16[16,1,4,6144]{3,2,1,0:T(4,128)(2,1)} async-done(((bf16[16,1,4,6144]{3,2,1,0:T(4,128)(2,1)}), bf16[16,1,4,6144]{3,2,1,0:T(4,128)(2,1)}, u32[]{:S(2)}, u32[]{:S(2)}) %all-to-all-start.6) | async-done | bytes 786464 | tf_op jit(solution)/shard_map/all_to_all | solution.py:111
  78.7 5.6 %all-to-all-start.4 = ((bf16[16,1,4,6144]{3,2,1,0:T(4,128)(2,1)}), bf16[16,1,4,6144]{3,2,1,0:T(4,128)(2,1)}, u32[]{:S(2)}, u32[]{:S(2)}) async-start(bf16[16,1,4,6144]{3,2,1,0:T(4,128)(2,1)} %reshape.273), calls=%async_computation.4 | async-start | bytes 1572864 | tf_op jit(solution)/shard_map/all_to_all | solution.py:111
  86.3 3.7 reshape.270
  91.0 3.7 reshape.267
  103.0 5.4 %all-to-all-start.2 = ((bf16[16,1,4,6144]{3,2,1,0:T(4,128)(2,1)}), bf16[16,1,4,6144]{3,2,1,0:T(4,128)(2,1)S(1)}, u32[]{:S(2)}, u32[]{:S(2)}) async-start(bf16[16,1,4,6144]{3,2,1,0:T(4,128)(2,1)} %reshape.270), calls=%async_computation.2 | async-start | bytes 1572864 | tf_op jit(solution)/shard_map/all_to_all | solution.py:111
  110.0 3.1 reshape.253
  134.7 6.4 %all-to-all-start = ((bf16[16,1,4,6144]{3,2,1,0:T(4,128)(2,1)}), bf16[16,1,4,6144]{3,2,1,0:T(4,128)(2,1)S(1)}, u32[]{:S(2)}, u32[]{:S(2)}) async-start(bf16[16,1,4,6144]{3,2,1,0:T(4,128)(2,1)} %reshape.267), calls=%async_computation | async-start | bytes 1572864 | tf_op jit(solution)/shard_map/all_to_all | solution.py:111
  142.5 4.3 reshape.252
  162.6 4.4 reshape.251
  207.8 5.1 %reshape.277 = bf16[16,1,4,6144]{3,2,1,0:T(4,128)(2,1)} reshape(bf16[16,4,128,48]{3,2,1,0:T(8,128)(2,1)} %copy.227) | data formatting | bytes 1572864 | tf_op jit(solution)/shard_map/reshape;transpose;reshape | solution.py:121
  212.9 6.1 %all-to-all-start.7 = ((bf16[16,1,4,6144]{3,2,1,0:T(4,128)(2,1)}), bf16[16,1,4,6144]{3,2,1,0:T(4,128)(2,1)}, u32[]{:S(2)}, u32[]{:S(2)}) async-start(bf16[16,1,4,6144]{3,2,1,0:T(4,128)(2,1)} %reshape.277), calls=%async_computation.7 | async-start | bytes 1572864 | tf_op jit(solution)/shard_map/all_to_all | solution.py:123
  317.4 5.1 %reshape.274 = bf16[16,1,4,6144]{3,2,1,0:T(4,128)(2,1)} reshape(bf16[16,4,128,48]{3,2,1,0:T(8,128)(2,1)} %copy.219) | data formatting | bytes 1572864 | tf_op jit(solution)/shard_map/reshape;transpose;reshape | solution.py:121
  325.3 5.3 %reshape.271 = bf16[16,1,4,6144]{3,2,1,0:T(4,128)(2,1)} reshape(bf16[16,4,128,48]{3,2,1,0:T(8,128)(2,1)} %copy.211) | data formatting | bytes 1572864 | tf_op jit(solution)/shard_map/reshape;transpose;reshape | solution.py:121
  338.3 6.1 %all-to-all-start.5 = ((bf16[16,1,4,6144]{3,2,1,0:T(4,128)(2,1)}), bf16[16,1,4,6144]{3,2,1,0:T(4,128)(2,1)}, u32[]{:S(2)}, u32[]{:S(2)}) async-start(bf16[16,1,4,6144]{3,2,1,0:T(4,128)(2,1)} %reshape.274), calls=%async_computation.5 | async-start | bytes 1572864 | tf_op jit(solution)/shard_map/all_to_all | solution.py:123
  353.2 10.0 %all-to-all-done.5 = bf16[16,1,4,6144]{3,2,1,0:T(4,128)(2,1)} async-done(((bf16[16,1,4,6144]{3,2,1,0:T(4,128)(2,1)}), bf16[16,1,4,6144]{3,2,1,0:T(4,128)(2,1)}, u32[]{:S(2)}, u32[]{:S(2)}) %all-to-all-start.5) | async-done | bytes 786464 | tf_op jit(solution)/shard_map/all_to_all | solution.py:123
  363.2 5.4 %all-to-all-start.3 = ((bf16[16,1,4,6144]{3,2,1,0:T(4,128)(2,1)}), bf16[16,1,4,6144]{3,2,1,0:T(4,128)(2,1)}, u32[]{:S(2)}, u32[]{:S(2)}) async-start(bf16[16,1,4,6144]{3,2,1,0:T(4,128)(2,1)} %reshape.271), calls=%async_computation.3 | async-start | bytes 1572864 | tf_op jit(solution)/shard_map/all_to_all | solution.py:123
  375.9 3.7 reshape.268
  379.6 7.8 %all-to-all-done.3 = bf16[16,1,4,6144]{3,2,1,0:T(4,128)(2,1)} async-done(((bf16[16,1,4,6144]{3,2,1,0:T(4,128)(2,1)}), bf16[16,1,4,6144]{3,2,1,0:T(4,128)(2,1)}, u32[]{:S(2)}, u32[]{:S(2)}) %all-to-all-start.3) | async-done | bytes 786464 | tf_op jit(solution)/shard_map/all_to_all | solution.py:123
  387.4 5.4 %all-to-all-start.1 = ((bf16[16,1,4,6144]{3,2,1,0:T(4,128)(2,1)}), bf16[16,1,4,6144]{3,2,1,0:T(4,128)(2,1)}, u32[]{:S(2)}, u32[]{:S(2)}) async-start(bf16[16,1,4,6144]{3,2,1,0:T(4,128)(2,1)} %reshape.268), calls=%async_computation.1 | async-start | bytes 1572864 | tf_op jit(solution)/shard_map/all_to_all | solution.py:123
  392.9 3.5 reshape.278
  397.3 3.3 reshape.275
  402.1 3.3 reshape.272
  406.9 4.6 all-to-all-done.1
  411.5 3.3 reshape.269
  418.2 7.0 %fusion = f32[16,48,768,1]{2,1,3,0:T(8,128)S(1)} fusion(bf16[16,4,128,768]{3,2,1,0:T(8,128)(2,1)} %gather_fusion, pred[16]{0:T(512)(128)(4,1)S(1)} %copy-done.96, bf16[4,4,128,16,48]{2,4,1,3,0:T(8,128)(2,1)S(1)} %maximum_bitcast_fusion.1), kind=kOutput, calls=%fused_computation.1 | convolution fusion | flops 610271232 | bytes 15729152 | tf_op jit(solution)/shard_map/rihj,rihe->jhe/dot_general | solution.py:141
  432.9 58.4 %reduce-scatter.2.cloned.1.call-done = f32[48,768]{1,0:T(8,128)} async-done(((f32[768,768]{1,0:T(8,128)}), f32[48,768]{1,0:T(8,128)}) %reduce-scatter.2.cloned.1.call-update) | async-done | bytes 147472 | tf_op jit(solution)/shard_map/reduce_scatter | solution.py:142
  (431 shorter events, 241.8 us)
Async XLA Ops:
  8.5 27.3 %copy-start.95 = (pred[16]{0:T(512)(128)(4,1)}, pred[16]{0:T(512)(128)(4,1)S(1)}, u32[]{:S(2)}) copy-start(pred[16]{0:T(512)(128)(4,1)S(1)} %compare_and_fusion) | copy-start | bytes 52
  10.9 12.7 %copy-start.72 = (bf16[4,128,768]{2,1,0:T(8,128)(2,1)S(1)}, bf16[4,128,768]{2,1,0:T(8,128)(2,1)}, u32[]{:S(2)}) copy-start(bf16[4,128,768]{2,1,0:T(8,128)(2,1)} %param.6) | copy-start | bytes 2359300
  10.9 13.1 %copy-start.73 = (bf16[4,128,768]{2,1,0:T(8,128)(2,1)S(1)}, bf16[4,128,768]{2,1,0:T(8,128)(2,1)}, u32[]{:S(2)}) copy-start(bf16[4,128,768]{2,1,0:T(8,128)(2,1)} %param.7) | copy-start | bytes 2359300
  10.9 13.5 %copy-start.74 = (bf16[4,128,768]{2,1,0:T(8,128)(2,1)S(1)}, bf16[4,128,768]{2,1,0:T(8,128)(2,1)}, u32[]{:S(2)}) copy-start(bf16[4,128,768]{2,1,0:T(8,128)(2,1)} %param.8) | copy-start | bytes 2359300
  52.5 26.2 %all-to-all-start.6 = ((bf16[16,1,4,6144]{3,2,1,0:T(4,128)(2,1)}), bf16[16,1,4,6144]{3,2,1,0:T(4,128)(2,1)}, u32[]{:S(2)}, u32[]{:S(2)}) async-start(bf16[16,1,4,6144]{3,2,1,0:T(4,128)(2,1)} %reshape.276), calls=%async_computation.6 | async-start | bytes 1572864 | tf_op jit(solution)/shard_map/all_to_all | solution.py:111
  78.7 24.3 %all-to-all-start.4 = ((bf16[16,1,4,6144]{3,2,1,0:T(4,128)(2,1)}), bf16[16,1,4,6144]{3,2,1,0:T(4,128)(2,1)}, u32[]{:S(2)}, u32[]{:S(2)}) async-start(bf16[16,1,4,6144]{3,2,1,0:T(4,128)(2,1)} %reshape.273), calls=%async_computation.4 | async-start | bytes 1572864 | tf_op jit(solution)/shard_map/all_to_all | solution.py:111
  101.9 30.1 %copy-start.19 = (bf16[1,16,128,48]{3,2,1,0:T(8,128)(2,1)}, bf16[1,16,128,48]{3,2,1,0:T(8,128)(2,1)S(1)}, u32[]{:S(2)}) copy-start(bf16[1,16,128,48]{3,2,1,0:T(8,128)(2,1)S(1)} %get-tuple-element.97) | copy-start | bytes 589828
  103.0 31.7 %all-to-all-start.2 = ((bf16[16,1,4,6144]{3,2,1,0:T(4,128)(2,1)}), bf16[16,1,4,6144]{3,2,1,0:T(4,128)(2,1)S(1)}, u32[]{:S(2)}, u32[]{:S(2)}) async-start(bf16[16,1,4,6144]{3,2,1,0:T(4,128)(2,1)} %reshape.270), calls=%async_computation.2 | async-start | bytes 1572864 | tf_op jit(solution)/shard_map/all_to_all | solution.py:111
  116.6 16.8 %copy-start.17 = (bf16[1,16,128,48]{3,2,1,0:T(8,128)(2,1)}, bf16[1,16,128,48]{3,2,1,0:T(8,128)(2,1)S(1)}, u32[]{:S(2)}) copy-start(bf16[1,16,128,48]{3,2,1,0:T(8,128)(2,1)S(1)} %get-tuple-element.87) | copy-start | bytes 589828
  119.1 3.9 copy-start.4
  125.6 5.1 %copy-start.10 = (f32[512,2048]{1,0:T(8,128)}, f32[512,2048]{1,0:T(8,128)S(1)}, u32[]{:S(2)}) copy-start(f32[512,2048]{1,0:T(8,128)S(1)} %fusion.20) | copy-start | bytes 12582916
  134.7 26.6 %all-to-all-start = ((bf16[16,1,4,6144]{3,2,1,0:T(4,128)(2,1)}), bf16[16,1,4,6144]{3,2,1,0:T(4,128)(2,1)S(1)}, u32[]{:S(2)}, u32[]{:S(2)}) async-start(bf16[16,1,4,6144]{3,2,1,0:T(4,128)(2,1)} %reshape.267), calls=%async_computation | async-start | bytes 1572864 | tf_op jit(solution)/shard_map/all_to_all | solution.py:111
  204.1 16.6 %copy-start.18 = (bf16[1,16,128,48]{3,2,1,0:T(8,128)(2,1)S(1)}, bf16[1,16,128,48]{3,2,1,0:T(8,128)(2,1)}, u32[]{:S(2)}) copy-start(bf16[1,16,128,48]{3,2,1,0:T(8,128)(2,1)} %copy-done.17) | copy-start | bytes 589828
  212.9 125.5 %all-to-all-start.7 = ((bf16[16,1,4,6144]{3,2,1,0:T(4,128)(2,1)}), bf16[16,1,4,6144]{3,2,1,0:T(4,128)(2,1)}, u32[]{:S(2)}, u32[]{:S(2)}) async-start(bf16[16,1,4,6144]{3,2,1,0:T(4,128)(2,1)} %reshape.277), calls=%async_computation.7 | async-start | bytes 1572864 | tf_op jit(solution)/shard_map/all_to_all | solution.py:123
  280.6 4.9 copy-start.48
  305.7 5.2 %copy-start.23 = (bf16[512,2048]{1,0:T(8,128)(2,1)}, bf16[512,2048]{1,0:T(8,128)(2,1)S(1)}, u32[]{:S(2)}) copy-start(bf16[512,2048]{1,0:T(8,128)(2,1)S(1)} %multiply_convert_fusion.14) | copy-start | bytes 6291460
  307.1 3.8 copy-start.51
  307.9 4.9 copy-start.25
  307.9 3.6 copy-start.49
  338.3 9.2 %copy-start.31 = (bf16[1,4,128,48]{3,2,1,0:T(8,128)(2,1)S(1)}, bf16[1,4,128,48]{3,2,1,0:T(8,128)(2,1)}, u32[]{:S(2)}) copy-start(bf16[1,4,128,48]{3,2,1,0:T(8,128)(2,1)} %get-tuple-element.65) | copy-start | bytes 147460
  338.3 24.9 %all-to-all-start.5 = ((bf16[16,1,4,6144]{3,2,1,0:T(4,128)(2,1)}), bf16[16,1,4,6144]{3,2,1,0:T(4,128)(2,1)}, u32[]{:S(2)}, u32[]{:S(2)}) async-start(bf16[16,1,4,6144]{3,2,1,0:T(4,128)(2,1)} %reshape.274), calls=%async_computation.5 | async-start | bytes 1572864 | tf_op jit(solution)/shard_map/all_to_all | solution.py:123
  344.5 5.9 %copy-start.3 = (f32[512,2048]{1,0:T(8,128)S(1)}, f32[512,2048]{1,0:T(8,128)}, u32[]{:S(2)}) copy-start(f32[512,2048]{1,0:T(8,128)} %fusion.6) | copy-start | bytes 12582916
  352.7 15.9 %copy-start.79 = (bf16[512,48]{0,1:T(8,128)(2,1)S(1)}, bf16[512,48]{0,1:T(8,128)(2,1)}, u32[]{:S(2)}) copy-start(bf16[512,48]{0,1:T(8,128)(2,1)} %get-tuple-element.156) | copy-start | bytes 147460
  352.7 16.0 %copy-start.80 = (bf16[512,48]{0,1:T(8,128)(2,1)S(1)}, bf16[512,48]{0,1:T(8,128)(2,1)}, u32[]{:S(2)}) copy-start(bf16[512,48]{0,1:T(8,128)(2,1)} %get-tuple-element.158) | copy-start | bytes 147460
  352.7 16.0 %copy-start.81 = (bf16[512,48]{0,1:T(8,128)(2,1)S(1)}, bf16[512,48]{0,1:T(8,128)(2,1)}, u32[]{:S(2)}) copy-start(bf16[512,48]{0,1:T(8,128)(2,1)} %get-tuple-element.160) | copy-start | bytes 147460
  352.7 17.1 %copy-start.75 = (bf16[6,8,16,128]{3,1,2,0:T(8,128)(2,1)S(1)}, bf16[6,8,16,128]{3,1,2,0:T(8,128)(2,1)}, u32[]{:S(2)}) copy-start(bf16[6,8,16,128]{3,1,2,0:T(8,128)(2,1)} %fusion.58) | copy-start | bytes 589828
  363.2 24.2 %all-to-all-start.3 = ((bf16[16,1,4,6144]{3,2,1,0:T(4,128)(2,1)}), bf16[16,1,4,6144]{3,2,1,0:T(4,128)(2,1)}, u32[]{:S(2)}, u32[]{:S(2)}) async-start(bf16[16,1,4,6144]{3,2,1,0:T(4,128)(2,1)} %reshape.271), calls=%async_computation.3 | async-start | bytes 1572864 | tf_op jit(solution)/shard_map/all_to_all | solution.py:123
  368.6 3.7 copy-start.26
  368.7 4.4 copy-start.24
  387.4 24.2 %all-to-all-start.1 = ((bf16[16,1,4,6144]{3,2,1,0:T(4,128)(2,1)}), bf16[16,1,4,6144]{3,2,1,0:T(4,128)(2,1)}, u32[]{:S(2)}, u32[]{:S(2)}) async-start(bf16[16,1,4,6144]{3,2,1,0:T(4,128)(2,1)} %reshape.268), calls=%async_computation.1 | async-start | bytes 1572864 | tf_op jit(solution)/shard_map/all_to_all | solution.py:123
  392.8 98.6 %reduce-scatter.2.cloned.1.call-start = ((), (), s32[]{:S(2)}) async-start(), calls=%async_computation.9 | async-start | bytes 2506752 | tf_op jit(solution)/shard_map/reduce_scatter | solution.py:142
  418.2 7.0 %copy-start.27 = (bf16[4,4,128,16,48]{2,4,1,3,0:T(8,128)(2,1)}, bf16[4,4,128,16,48]{2,4,1,3,0:T(8,128)(2,1)S(1)}, u32[]{:S(2)}) copy-start(bf16[4,4,128,16,48]{2,4,1,3,0:T(8,128)(2,1)S(1)} %maximum_bitcast_fusion.1) | copy-start | bytes 9437188
  (74 other events, 163.2 us)
Sparse Core Ops, SparseCore 0:
  427.4 63.9 reduce-scatter.1
where the time goes:
time: 508 us; the launch traced here: 498 us
  local copies, waits for them, and re-layouts  176 us (35%)
  matrix products  111 us (22%)
  waiting for transfers between devices  95 us (19%)
  other arithmetic  52.1 us (10%)
  starting transfers between devices  48.1 us (9%)
  between operations  16.2 us (3%)
    reduce_scatter x1, waiting for transfers between devices, local(): lax.psum_scatter(term.reshape(feature_width // tok_count * lax.axis_size(...  58.4 us
    div x16, other arithmetic, attend(): probs = expo / jnp.sum(expo, axis=1, keepdims=True)  30.9 us
    another operation x8, local copies, waits for them, and re-layouts, local(): results = results.reshape(groups, count, heads, 4, flat_size).transpose(0...  28.4 us
    unnamed x217, local copies, waits for them, and re-layouts  25.7 us
    all_to_all x4, starting transfers between devices, local(): lax.all_to_all(sending, 'tok', split_axis=0, concat_axis=0, tiled=True)  24.9 us
    all_to_all x4, starting transfers between devices, local(): lax.all_to_all(shortened(results), 'tok', split_axis=0, concat_axis=0, ti...  23.1 us
    all_to_all x4, waiting for transfers between devices, local(): lax.all_to_all(shortened(results), 'tok', split_axis=0, concat_axis=0, ti...  22.4 us
    another operation x8, local copies, waits for them, and re-layouts, local(): sending = block_rounds.reshape(groups, count, heads, 4, flat_size).transp...  21.7 us
  transfers between devices with their start and end apart: 9, of which 6 were waited for; matrix products, arithmetic and copies ran while one was open for 43% of the time, Pallas kernels for 0%

commit v1 on v0

v1 whole, which is shorter than its diff:
```python
import functools

import jax
import jax.numpy as jnp
from jax import lax
from jax.experimental import pallas as pl
from jax.experimental.pallas import tpu as pltpu
from jax.sharding import PartitionSpec as P

MESH = pl.DeviceIdType.MESH
F32 = jnp.float32
BF16 = jnp.bfloat16
LOG2E = 1.4426950408889634


def dot(a, b, ca, cb):
    return lax.dot_general(a, b, (((ca,), (cb,)), ((), ())), preferred_element_type=F32)


def flip_bits(index, mask):
    out = index
    bit = 1
    while bit <= mask:
        if mask & bit:
            out = out + bit - 2 * bit * ((index // bit) % 2)
        bit *= 2
    return out


def main_kernel(
    dims,
    q_ref, k_ref, v_ref, w_ref, mask_ref, x_hbm,
    dq_ref, dk_ref, dv_ref, gw_ref,
    x, out_t, recv, res, ret, g_rows, spread, k_rows, v_rows, dk_acc, dv_acc, term, half, part, landed,
    x_sem, qkv_send, qkv_recv, g_send, g_recv, res_send, ret_recv, red_send, red_recv,
):
    rounds, rows, width, heads, head_dim, tok, phases = dims
    seg = heads * rows
    me = lax.axis_index("tok")
    lane = me % heads
    base = me - lane
    order = sorted(range(1, heads), key=lambda s: (-(s // (heads // 2)), -s))
    scale = head_dim ** (-0.5)

    for r in range(rounds):
        pltpu.make_async_copy(x_hbm.at[r], x.at[r], x_sem.at[r]).start()

    greet = sorted(set(flip_bits_plain(heads)) | set(b for b in bits_of(tok)))
    barrier = pltpu.get_barrier_semaphore()
    for s in greet:
        peer = flip_bits(me, s)
        pl.semaphore_signal(barrier, inc=1, device_id={"tok": peer}, device_id_type=MESH)
    pl.semaphore_wait(barrier, len(greet))

    def columns(d):
        return pl.ds(pl.multiple_of(d * rows, rows), rows)

    def send_out(r, first, count, send_sem, recv_sem):
        for s in order:
            d = flip_bits(lane, s)
            pltpu.make_async_remote_copy(
                src_ref=out_t.at[r, pl.ds(first, count), d],
                dst_ref=recv.at[r, pl.ds(first, count), :, columns(lane)],
                send_sem=send_sem.at[r],
                recv_sem=recv_sem.at[r],
                device_id={"tok": base + d},
                device_id_type=MESH,
            ).start()
        pltpu.make_async_copy(
            out_t.at[r, pl.ds(first, count), lane],
            recv.at[r, pl.ds(first, count), :, columns(lane)],
            recv_sem.at[r],
        ).start()

    def prepare(r, carry):
        for a, ref in enumerate((q_ref, k_ref, v_ref)):
            out_t[r, a] = ref[r].T.reshape(heads, head_dim, rows)
        send_out(r, 0, 3, qkv_send, qkv_recv)
        pltpu.make_async_copy(x_hbm.at[r], x.at[r], x_sem.at[r]).wait()

        def chunk(c, inner):
            t = pl.multiple_of(c * 256, 256)
            y = dot(x[r, pl.ds(t, 256), :], w_ref[...], 1, 0)
            y = y.reshape(256 // phases, phases, width) * mask_ref[...][None]
            i = pl.multiple_of(c * (256 // phases), 256 // phases)
            g_rows[pl.ds(i, 256 // phases), :] = jnp.sum(y, axis=1).astype(BF16)
            return inner

        lax.fori_loop(0, rows * phases // 256, chunk, 0)
        out_t[r, 3] = g_rows[...].T.reshape(heads, head_dim, rows)
        send_out(r, 3, 1, g_send, g_recv)
        return carry

    lax.fori_loop(0, rounds, prepare, 0)

    block = 256

    def attend(r, carry):
        pltpu.make_async_copy(
            recv.at[r, pl.ds(0, 3)], recv.at[r, pl.ds(0, 3)], qkv_recv.at[r]
        ).wait()
        k_rows[...] = recv[r, 1].T
        v_rows[...] = recv[r, 2].T
        dk_acc[...] = jnp.zeros_like(dk_acc)
        dv_acc[...] = jnp.zeros_like(dv_acc)
        pltpu.make_async_copy(recv.at[r, 3], recv.at[r, 3], g_recv.at[r]).wait()

        def q_block(b, inner):
            cols = pl.ds(pl.multiple_of(b * block, block), block)
            qt = recv[r, 0, :, cols]
            gt = recv[r, 3, :, cols]
            s = dot(k_rows[...], qt, 1, 0)
            top = jnp.max(s, axis=0, keepdims=True)
            e = jnp.exp2((s - top) * (scale * LOG2E))
            inv = 1.0 / jnp.sum(e, axis=0, keepdims=True)
            p = e * inv
            p_low = p.astype(BF16)
            ot = dot(recv[r, 2], p_low, 1, 0).astype(BF16)
            res[r, 3, :, cols] = ot
            dp = dot(v_rows[...], gt, 1, 0)
            delta = jnp.sum(gt.astype(F32) * ot.astype(F32), axis=0, keepdims=True)
            ds = (p * (dp - delta)).astype(BF16)
            res[r, 0, :, cols] = (dot(recv[r, 1], ds, 1, 0) * scale).astype(BF16)
            dk_acc[...] += dot(qt, ds, 1, 1)
            dv_acc[...] += dot(gt, p_low, 1, 1)
            return inner

        lax.fori_loop(0, seg // block, q_block, 0)
        res[r, 1] = (dk_acc[...] * scale).astype(BF16)
        res[r, 2] = dv_acc[...].astype(BF16)
        for s in order:
            d = flip_bits(lane, s)
            pltpu.make_async_remote_copy(
                src_ref=res.at[r, :, :, columns(d)],
                dst_ref=ret.at[r, :, lane],
                send_sem=res_send.at[r],
                recv_sem=ret_recv.at[r],
                device_id={"tok": base + d},
                device_id_type=MESH,
            ).start()
        pltpu.make_async_copy(
            res.at[r, :, :, columns(lane)], ret.at[r, :, lane], ret_recv.at[r]
        ).start()
        return carry

    lax.fori_loop(0, rounds, attend, 0)

    term[...] = jnp.zeros_like(term)
    jb = 256

    def finish(r, carry):
        pltpu.make_async_copy(ret.at[r], ret.at[r], ret_recv.at[r]).wait()
        g_rows[...] = ret[r, 3].reshape(width, rows).T

        def chunk(c, inner):
            n = 256 // phases
            a = g_rows[pl.ds(pl.multiple_of(c * n, n), n), :].astype(F32)
            full = a[:, None, :] * mask_ref[...][None]
            spread[pl.ds(pl.multiple_of(c * 256, 256), 256), :] = full.reshape(256, width).astype(BF16)
            return inner

        lax.fori_loop(0, rows * phases // 256, chunk, 0)

        for j in range(width // jb):
            here = pl.ds(j * jb, jb)
            term[here, :] += dot(x[r, :, here], spread[...], 0, 0)
        for a, ref in enumerate((dq_ref, dk_ref, dv_ref)):
            ref[r] = ret[r, a].reshape(width, rows).T
        return carry

    lax.fori_loop(0, rounds, finish, 0)

    own = width // tok
    part[...] = term[...].reshape(tok, own, width)
    count = tok
    stage = 0
    bit = 1
    at = 0
    kept = 0
    while bit < tok:
        b = (me // bit) % 2
        peer = me + bit - 2 * bit * b
        count //= 2
        for u in range(count):
            half[at + u] = part[kept + bit * (1 - b) + 2 * bit * u].astype(BF16)
        for u in range(count):
            pltpu.make_async_remote_copy(
                src_ref=half.at[at + u],
                dst_ref=landed.at[at + u],
                send_sem=red_send.at[at + u],
                recv_sem=red_recv.at[at + u],
                device_id={"tok": peer},
                device_id_type=MESH,
            ).start()
        kept = kept + bit * b
        for u in range(count):
            pltpu.make_async_remote_copy(
                src_ref=half.at[at + u],
                dst_ref=landed.at[at + u],
                send_sem=red_send.at[at + u],
                recv_sem=red_recv.at[at + u],
                device_id={"tok": peer},
                device_id_type=MESH,
            ).wait()
            part[kept + 2 * bit * u] += landed[at + u].astype(F32)
        at += count
        bit *= 2
    gw_ref[...] = part[me]

    for r in range(rounds):
        blocks = pl.ds(0, heads - 1)
        sent = out_t.at[r, pl.ds(0, 3), blocks]
        pltpu.make_async_copy(sent, sent, qkv_send.at[r]).wait()
        sent = out_t.at[r, pl.ds(3, 1), blocks]
        pltpu.make_async_copy(sent, sent, g_send.at[r]).wait()
        sent = ret.at[r, :, blocks]
        pltpu.make_async_copy(sent, sent, res_send.at[r]).wait()


def flip_bits_plain(heads):
    return range(1, heads)


def bits_of(tok):
    bit = 1
    while bit < tok:
        yield bit
        bit *= 2


def local(queries, key_rows, value_rows, projected_output_gradient, out_weight, offsets):
    rounds, rows, width = queries.shape
    heads = offsets.shape[0]
    head_dim = width // heads
    tok = lax.axis_size("tok")
    phases = projected_output_gradient.shape[1] // rows
    seg = heads * rows
    own = width // tok
    dims = (rounds, rows, width, heads, head_dim, tok, phases)
    mask = (jnp.arange(phases)[:, None] == jnp.repeat(offsets, head_dim)[None, :]).astype(F32)
    vmem = pl.BlockSpec(memory_space=pltpu.VMEM)
    rows_shape = jax.ShapeDtypeStruct((rounds, rows, width), BF16)
    return pl.pallas_call(
        functools.partial(main_kernel, dims),
        out_shape=(rows_shape, rows_shape, rows_shape, jax.ShapeDtypeStruct((own, width), F32)),
        in_specs=[vmem] * 5 + [pl.BlockSpec(memory_space=pl.ANY)],
        out_specs=(vmem,) * 4,
        scratch_shapes=[
            pltpu.VMEM((rounds, rows * phases, width), BF16),
            pltpu.VMEM((rounds, 4, heads, head_dim, rows), BF16),
            pltpu.VMEM((rounds, 4, head_dim, seg), BF16),
            pltpu.VMEM((rounds, 4, head_dim, seg), BF16),
            pltpu.VMEM((rounds, 4, heads, head_dim, rows), BF16),
            pltpu.VMEM((rows, width), BF16),
            pltpu.VMEM((rows * phases, width), BF16),
            pltpu.VMEM((seg, head_dim), BF16),
            pltpu.VMEM((seg, head_dim), BF16),
            pltpu.VMEM((head_dim, seg), F32),
            pltpu.VMEM((head_dim, seg), F32),
            pltpu.VMEM((width, width), F32),
            pltpu.VMEM((tok, own, width), BF16),
            pltpu.VMEM((tok, own, width), F32),
            pltpu.VMEM((tok, own, width), BF16),
            pltpu.SemaphoreType.DMA((rounds,)),
            pltpu.SemaphoreType.DMA((rounds,)),
            pltpu.SemaphoreType.DMA((rounds,)),
            pltpu.SemaphoreType.DMA((rounds,)),
            pltpu.SemaphoreType.DMA((rounds,)),
            pltpu.SemaphoreType.DMA((rounds,)),
            pltpu.SemaphoreType.DMA((rounds,)),
            pltpu.SemaphoreType.DMA((tok,)),
            pltpu.SemaphoreType.DMA((tok,)),
        ],
        compiler_params=pltpu.CompilerParams(
            collective_id=0, has_side_effects=True, vmem_limit_bytes=64000000
        ),
        name="branch_backward",
    )(queries, key_rows, value_rows, out_weight, mask, projected_output_gradient)


def solution(mesh):
    placed = (
        P("slides", "tok", None),
        P("slides", "tok", None),
        P("slides", "tok", None),
        P("slides", "tok", None),
        P(),
        P(),
    )
    return jax.shard_map(
        local,
        mesh=mesh,
        in_specs=placed,
        out_specs=(
            P("slides", "tok", None),
            P("slides", "tok", None),
            P("slides", "tok", None),
            P(("slides", "tok"), None),
        ),
        check_vma=False,
    )
```

time: 508 us -> 180 us (0.35); the launches traced: 498 us -> 179 us
  Pallas kernels: 0 us -> 169 us
  local copies, waits for them, and re-layouts: 176 us -> 8.57 us
  matrix products: 111 us -> 0 us
  waiting for transfers between devices: 95 us -> 0 us
  other arithmetic: 52.1 us -> 0.63 us
  starting transfers between devices: 48.1 us -> 0 us
  between operations: 16.2 us -> 0.64 us
    pallas_call x0 -> x1, Pallas kernels: none -> 169 us  [local(): pl.pallas_call(functools.partial(main_kernel, dims), out_shape=(rows_shap...]
    dot_general x98 -> x0, matrix products: 111 us -> none  [the longest x16 20.6 us: attend(): jnp.einsum('qe,ke->qk', query_part, key_all, preferred_element_type=jnp.f...]
    reduce_scatter x1 -> x0, waiting for transfers between devices: 58.4 us -> none  [local(): lax.psum_scatter(term.reshape(feature_width // tok_count * lax.axis_size(...]
    another operation x32 -> x0, local copies, waits for them, and re-layouts: 56.2 us -> none  [the longest x8 28.4 us: local(): results = results.reshape(groups, count, heads, 4, flat_size).transpose(0...]
    all_to_all x8 -> x0, starting transfers between devices: 48 us -> none  [the longest x4 24.9 us: local(): lax.all_to_all(sending, 'tok', split_axis=0, concat_axis=0, tiled=True)]
    all_to_all x8 -> x0, waiting for transfers between devices: 36.5 us -> none  [the longest x4 22.4 us: local(): lax.all_to_all(shortened(results), 'tok', split_axis=0, concat_axis=0, ti...]
    div x16 -> x0, other arithmetic: 30.9 us -> none  [attend(): probs = expo / jnp.sum(expo, axis=1, keepdims=True)]
    slice x29 -> x0, local copies, waits for them, and re-layouts: 29.5 us -> none  [the longest x20 20.4 us: attend(): grad_part = grad_all[first_row:first_row + block_rows]]
  transfers between devices with their start and end apart: 9 -> 0, of which waited for: 6 -> 0; matrix products, arithmetic and copies ran while one was open for 43% -> 0% of each run, Pallas kernels for 0% -> 0%
where the time goes in v1:
time: 180 us; the launch traced here: 179 us
  Pallas kernels  169 us (94%)
  local copies, waits for them, and re-layouts  8.57 us (5%)
    pallas_call x1, Pallas kernels, local(): pl.pallas_call(functools.partial(main_kernel, dims), out_shape=(rows_shap...  169 us
    unnamed x4, local copies, waits for them, and re-layouts  7.77 us

profile of v1, /device:TPU:0, one launch (start us, length us, event | category | flops | bytes accessed | tf_op | source)
XLA Modules:
  0.0 179.3 jit_solution(17249740242158874049)
XLA Ops:
  0.6 0.7 broadcast_in_dim.4
  1.4 0.1 eq.16
  1.4 0.6 fusion.mask_ref
  2.1 169.4 %branch_backward.1 = (bf16[4,128,768]{2,1,0:T(8,128)(2,1)}, bf16[4,128,768]{2,1,0:T(8,128)(2,1)}, bf16[4,128,768]{2,1,0:T(8,128)(2,1)}, f32[48,768]{1,0:T(8,128)}) custom-call(bf16[4,128,768]{2,1,0:T(8,128)(2,1)} %q_ref.1, bf16[4,128,768]{2,1,0:T(8,128)(2,1)} %k_ref.1, bf16[4,128,768]{2,1,0:T(8,128)(2,1)} %v_ref.1, bf16[768,768]{1,0:T(8,128)(2,1)} %w_ref.1, ...), custom_call_target="tpu_custom_call" | custom-call | tf_op jit(solution)/shard_map/branch_backward/pallas_call | solution.py:243
  171.5 2.1 %copy.14 = bf16[4,128,768]{2,1,0:T(8,128)(2,1)} copy(bf16[4,128,768]{2,1,0:T(8,128)(2,1)} %get-tuple-element.8) | data formatting | bytes 1572864
  173.6 2.1 %copy.15 = bf16[4,128,768]{2,1,0:T(8,128)(2,1)} copy(bf16[4,128,768]{2,1,0:T(8,128)(2,1)} %get-tuple-element.9) | data formatting | bytes 1572864
  175.6 2.1 %copy.16 = bf16[4,128,768]{2,1,0:T(8,128)(2,1)} copy(bf16[4,128,768]{2,1,0:T(8,128)(2,1)} %get-tuple-element.10) | data formatting | bytes 1572864
  177.7 1.6 copy.17

commit v2 on v1

--- a/solution.py
+++ b/solution.py
@@ -32,7 +32,7 @@
     q_ref, k_ref, v_ref, w_ref, mask_ref, x_hbm,
     dq_ref, dk_ref, dv_ref, gw_ref,
     x, out_t, recv, res, ret, g_rows, spread, k_rows, v_rows, dk_acc, dv_acc, term, half, part, landed,
-    x_sem, qkv_send, qkv_recv, g_send, g_recv, res_send, ret_recv, red_send, red_recv,
+    x_sem, qkv_send, qkv_recv, g_send, g_recv, res_send, ret_recv, attn_send, attn_recv, red_send, red_recv,
 ):
     rounds, rows, width, heads, head_dim, tok, phases = dims
     seg = heads * rows
@@ -92,6 +92,23 @@
         return carry
 
     lax.fori_loop(0, rounds, prepare, 0)
+
+    def send_back(r, first, count, send_sem, recv_sem):
+        for s in order:
+            d = flip_bits(lane, s)
+            pltpu.make_async_remote_copy(
+                src_ref=res.at[r, pl.ds(first, count), :, columns(d)],
+                dst_ref=ret.at[r, pl.ds(first, count), lane],
+                send_sem=send_sem.at[r],
+                recv_sem=recv_sem.at[r],
+                device_id={"tok": base + d},
+                device_id_type=MESH,
+            ).start()
+        pltpu.make_async_copy(
+            res.at[r, pl.ds(first, count), :, columns(lane)],
+            ret.at[r, pl.ds(first, count), lane],
+            recv_sem.at[r],
+        ).start()
 
     block = 256
 
@@ -128,19 +145,8 @@
         lax.fori_loop(0, seg // block, q_block, 0)
         res[r, 1] = (dk_acc[...] * scale).astype(BF16)
         res[r, 2] = dv_acc[...].astype(BF16)
-        for s in order:
-            d = flip_bits(lane, s)
-            pltpu.make_async_remote_copy(
-                src_ref=res.at[r, :, :, columns(d)],
-                dst_ref=ret.at[r, :, lane],
-                send_sem=res_send.at[r],
-                recv_sem=ret_recv.at[r],
-                device_id={"tok": base + d},
-                device_id_type=MESH,
-            ).start()
-        pltpu.make_async_copy(
-            res.at[r, :, :, columns(lane)], ret.at[r, :, lane], ret_recv.at[r]
-        ).start()
+        send_back(r, 3, 1, attn_send, attn_recv)
+        send_back(r, 0, 3, res_send, ret_recv)
         return carry
 
     lax.fori_loop(0, rounds, attend, 0)
@@ -149,7 +155,7 @@
     jb = 256
 
     def finish(r, carry):
-        pltpu.make_async_copy(ret.at[r], ret.at[r], ret_recv.at[r]).wait()
+        pltpu.make_async_copy(ret.at[r, 3], ret.at[r, 3], attn_recv.at[r]).wait()
         g_rows[...] = ret[r, 3].reshape(width, rows).T
 
         def chunk(c, inner):
@@ -164,11 +170,18 @@
         for j in range(width // jb):
             here = pl.ds(j * jb, jb)
             term[here, :] += dot(x[r, :, here], spread[...], 0, 0)
+        return carry
+
+    lax.fori_loop(0, rounds, finish, 0)
+
+    def lay_out(r, carry):
+        got = ret.at[r, pl.ds(0, 3)]
+        pltpu.make_async_copy(got, got, ret_recv.at[r]).wait()
         for a, ref in enumerate((dq_ref, dk_ref, dv_ref)):
             ref[r] = ret[r, a].reshape(width, rows).T
         return carry
 
-    lax.fori_loop(0, rounds, finish, 0)
+    lax.fori_loop(0, rounds - 1, lay_out, 0)
 
     own = width // tok
     part[...] = term[...].reshape(tok, own, width)
@@ -193,6 +206,8 @@
                 device_id_type=MESH,
             ).start()
         kept = kept + bit * b
+        if bit == 1:
+            lay_out(rounds - 1, 0)
         for u in range(count):
             pltpu.make_async_remote_copy(
                 src_ref=half.at[at + u],
@@ -213,8 +228,10 @@
         pltpu.make_async_copy(sent, sent, qkv_send.at[r]).wait()
         sent = out_t.at[r, pl.ds(3, 1), blocks]
         pltpu.make_async_copy(sent, sent, g_send.at[r]).wait()
-        sent = ret.at[r, :, blocks]
+        sent = ret.at[r, pl.ds(0, 3), blocks]
         pltpu.make_async_copy(sent, sent, res_send.at[r]).wait()
+        sent = ret.at[r, pl.ds(3, 1), blocks]
+        pltpu.make_async_copy(sent, sent, attn_send.at[r]).wait()
 
 
 def flip_bits_plain(heads):
@@ -268,6 +285,8 @@
             pltpu.SemaphoreType.DMA((rounds,)),
             pltpu.SemaphoreType.DMA((rounds,)),
             pltpu.SemaphoreType.DMA((rounds,)),
+            pltpu.SemaphoreType.DMA((rounds,)),
+            pltpu.SemaphoreType.DMA((rounds,)),
             pltpu.SemaphoreType.DMA((tok,)),
             pltpu.SemaphoreType.DMA((tok,)),
         ],

time: 180 us -> 174 us (0.967)
  Pallas kernels: 169 us -> 164 us
    pallas_call x1, Pallas kernels: 169 us -> 164 us  [local(): pl.pallas_call(functools.partial(main_kernel, dims), out_shape=(rows_shap...]
where the time goes in v2:
time: 174 us
  Pallas kernels  164 us (94%)
  local copies, waits for them, and re-layouts  8.57 us (5%)
    pallas_call x1, Pallas kernels, local(): pl.pallas_call(functools.partial(main_kernel, dims), out_shape=(rows_shap...  164 us
    unnamed x4, local copies, waits for them, and re-layouts  7.77 us

profile of v2, /device:TPU:0, one launch (start us, length us, event | category | flops | bytes accessed | tf_op | source)
XLA Modules:
  0.0 173.6 jit_solution(10807166356333272651)
XLA Ops:
  0.6 0.7 broadcast_in_dim.4
  1.4 0.1 eq.16
  1.4 0.6 fusion.mask_ref
  2.1 163.8 %branch_backward.1 = (bf16[4,128,768]{2,1,0:T(8,128)(2,1)}, bf16[4,128,768]{2,1,0:T(8,128)(2,1)}, bf16[4,128,768]{2,1,0:T(8,128)(2,1)}, f32[48,768]{1,0:T(8,128)}) custom-call(bf16[4,128,768]{2,1,0:T(8,128)(2,1)} %q_ref.1, bf16[4,128,768]{2,1,0:T(8,128)(2,1)} %k_ref.1, bf16[4,128,768]{2,1,0:T(8,128)(2,1)} %v_ref.1, bf16[768,768]{1,0:T(8,128)(2,1)} %w_ref.1, ...), custom_call_target="tpu_custom_call" | custom-call | tf_op jit(solution)/shard_map/branch_backward/pallas_call | solution.py:260
  165.9 2.1 %copy.14 = bf16[4,128,768]{2,1,0:T(8,128)(2,1)} copy(bf16[4,128,768]{2,1,0:T(8,128)(2,1)} %get-tuple-element.8) | data formatting | bytes 1572864
  167.9 2.1 %copy.15 = bf16[4,128,768]{2,1,0:T(8,128)(2,1)} copy(bf16[4,128,768]{2,1,0:T(8,128)(2,1)} %get-tuple-element.9) | data formatting | bytes 1572864
  170.0 2.1 %copy.16 = bf16[4,128,768]{2,1,0:T(8,128)(2,1)} copy(bf16[4,128,768]{2,1,0:T(8,128)(2,1)} %get-tuple-element.10) | data formatting | bytes 1572864
  172.1 1.6 copy.17
